TPU v7x, 128 devices: a whole 4x4x4 slice. The times are simulated.
128 devices in a mesh: rows: 8 (over z, core), cols: 16 (over y, x).
Axes of the slice: x: 4, y: 4, z: 4, core: 2. Of those that a mesh axis runs over, the one named last changes fastest.
Arguments:
- model_dir: float32 [131072, 128], P('cols'), may hold values from -6 to 6
- sens_blocks: bfloat16 [8, 6144, 128, 128], P('rows', 'cols'), may hold values from -0.0625 to 0.0625
- blk_row: int32 [8, 6144], P('rows', 'cols'), may hold values from 0 to 31, as said below
- blk_col: int32 [8, 6144], P('rows', 'cols'), may hold values from 0 to 63, as said below
- blk_count: int32 [8, 16], P('rows', 'cols'), may hold values from 48 to 384, as said below
- send_order: int32 [16, 64], P('cols'), may hold values from 0 to 63, each once within a row
- neighbors: int32 [4, 131072], P(None, 'cols'), may hold values from 0 to 131071, as said below
- face_weight: float32 [4, 131072], P(None, 'cols'), may hold values from 0.05 to 0.5
Outputs:
- data_image: float32 [32768, 128], P('rows')
- normal_product: float32 [131072, 128], P('cols')
Inputs may be any that keep to these rules, and one draw needn't show every extreme that they name: Within one device's 384 slots the pairs (blk_row, blk_col) are all different. `blk_col`: paired with blk_row as stated there. The live slots of a device are its first blk_count slots; some device has all 384 live. `send_order`: each row is a permutation. `neighbors`: every neighbour lies within 64 of the cell's own number.
All inputs are finite; a program needn't handle non-finite values.
Results may differ from a plain program's by a relative error of at most 0.0029.
Values may be sent and summed in bfloat16 or wider, within the bound.
A program may use at most 192 MiB of HBM per device.

v0:
```python
import math
import jax
import jax.numpy as jnp
from jax import lax
from jax.sharding import PartitionSpec as P

BLK = 128
RB_DEV = 32
RIM = 64


def padded_2(block, sides, width):
    for axis, dim in sides:
        count = lax.axis_size(axis)
        forward = [(i, i + 1) for i in range(count - 1)]
        backward = [(target, source) for source, target in forward]
        low = lax.ppermute(
            lax.slice_in_dim(block, block.shape[dim] - width, None, axis=dim), axis, forward
        )
        high = lax.ppermute(lax.slice_in_dim(block, 0, width, axis=dim), axis, backward)
        block = jnp.concatenate([low, block, high], axis=dim)
    return block


def haar_matrix(order_n):
    matrix = jnp.ones((1, 1), jnp.float32)
    factor = 1.0 / math.sqrt(2.0)
    while matrix.shape[0] < order_n:
        length = matrix.shape[0]
        upper_half = jnp.kron(matrix, jnp.array([[1.0, 1.0]], jnp.float32))
        lower_half = jnp.kron(
            jnp.eye(length, dtype=jnp.float32), jnp.array([[1.0, -1.0]], jnp.float32)
        )
        matrix = jnp.concatenate([upper_half, lower_half], axis=0) * factor
    return matrix


def one_hot(indices, length, dtype):
    return (indices[:, None] == lax.iota(jnp.int32, length)[None, :]).astype(dtype)


def smoothing(extended, center, neighbors, face_weight, offset):
    cell_count, width = center.shape
    tile_count = cell_count // BLK
    tiles = extended.reshape(tile_count + 1, BLK, width)
    window = jnp.concatenate([tiles[:-1], tiles[1:]], axis=1)
    starts = lax.iota(jnp.int32, tile_count) * BLK
    local_index = (neighbors - offset).reshape(4, tile_count, BLK) - starts[None, :, None]
    span = lax.iota(jnp.int32, 2 * BLK)
    weights = jnp.zeros((tile_count, BLK, 2 * BLK), jnp.float32)
    for face in range(4):
        face_w = face_weight[face].reshape(tile_count, BLK)
        weights = weights + jnp.where(
            local_index[face][:, :, None] == span[None, None, :], face_w[:, :, None], 0.0
        )
    mixed = jnp.einsum("bij,bjn->bin", weights, window, precision=lax.Precision.HIGHEST)
    total_w = jnp.sum(face_weight, axis=0)
    return total_w[:, None] * center - mixed.reshape(cell_count, width)


def synthesize(haar_basis, returned, send_onehot, block_count, cell_count):
    share_cols = returned.shape[-1]
    flat_back = returned.reshape(block_count, BLK * share_cols)
    cell_side = jnp.einsum("jb,jm->bm", send_onehot, flat_back, precision=lax.Precision.HIGHEST)
    cell_side = cell_side.reshape(block_count, BLK, share_cols)
    result = jnp.einsum("ji,bjn->bin", haar_basis, cell_side, precision=lax.Precision.HIGHEST)
    return result.reshape(cell_count, share_cols)


def local(model_dir, sens_blocks, blk_row, blk_col, blk_count, send_order, neighbors, face_weight):
    highest = lax.Precision.HIGHEST
    cell_count, vec_width = model_dir.shape
    block_count = cell_count // BLK
    col_devices = lax.axis_size("cols")
    per_peer = block_count // col_devices
    haar_basis = jnp.asarray(haar_matrix(BLK), jnp.float32)
    cell_blocks = model_dir.reshape(block_count, BLK, vec_width)
    coeffs = jnp.einsum("ij,bjn->bin", haar_basis, cell_blocks, precision=highest).astype(
        jnp.bfloat16
    )
    order_here = send_order[0]
    send_half = one_hot(order_here, block_count, jnp.bfloat16)
    ordered = jnp.dot(
        send_half, coeffs.reshape(block_count, BLK * vec_width), preferred_element_type=jnp.float32
    )
    outgoing = ordered.astype(jnp.bfloat16).reshape(col_devices, per_peer * BLK, vec_width)
    wavelet = lax.all_to_all(outgoing, "cols", split_axis=0, concat_axis=0, tiled=True).reshape(
        block_count, BLK * vec_width
    )
    rows_here = blk_row[0]
    cols_here = blk_col[0]
    sensors = sens_blocks[0]
    slot_count = sensors.shape[0]
    live_slot = lax.iota(jnp.int32, slot_count) < blk_count[0, 0]
    pick_cols = one_hot(cols_here, block_count, jnp.bfloat16)
    picked = jnp.dot(pick_cols, wavelet, preferred_element_type=jnp.float32).astype(jnp.bfloat16)
    picked = picked.reshape(slot_count, BLK, vec_width)
    forward = jnp.einsum("kij,kjn->kin", sensors, picked, preferred_element_type=jnp.float32)
    row_mask = (one_hot(rows_here, RB_DEV, jnp.float32) * live_slot[:, None].astype(jnp.float32)).T
    partial_rows = jnp.dot(
        row_mask, forward.reshape(slot_count, BLK * vec_width), precision=highest
    )
    partial_rows = partial_rows.reshape(RB_DEV, BLK, vec_width)
    predicted = lax.psum(partial_rows, "cols")
    data_image = predicted.reshape(RB_DEV * BLK, vec_width)
    image_half = predicted.astype(jnp.bfloat16).reshape(RB_DEV, BLK * vec_width)
    pick_rows = one_hot(rows_here, RB_DEV, jnp.bfloat16)
    chosen = jnp.dot(pick_rows, image_half, preferred_element_type=jnp.float32).astype(jnp.bfloat16)
    chosen = chosen.reshape(slot_count, BLK, vec_width)
    adjoint = jnp.einsum("kij,kin->kjn", sensors, chosen, preferred_element_type=jnp.float32)
    col_mask = (
        one_hot(cols_here, block_count, jnp.float32) * live_slot[:, None].astype(jnp.float32)
    ).T
    partial_cols = jnp.dot(
        col_mask, adjoint.reshape(slot_count, BLK * vec_width), precision=highest
    )
    partial_cols = partial_cols.reshape(block_count, BLK, vec_width)
    extended = padded_2(model_dir, (("cols", 0),), RIM)
    offset = lax.axis_index("cols") * cell_count - RIM
    send_full = one_hot(order_here, block_count, jnp.float32)
    summed = lax.psum(partial_cols, "rows")
    returned = lax.all_to_all(
        summed.reshape(col_devices, per_peer * BLK, vec_width),
        "cols",
        split_axis=0,
        concat_axis=0,
        tiled=True,
    )
    synthesis = synthesize(haar_basis, returned, send_full, block_count, cell_count)
    normal_product = synthesis + smoothing(extended, model_dir, neighbors, face_weight, offset)
    return (data_image, normal_product)


def solution(mesh):
    placed = (
        P("cols", None),
        P("rows", "cols", None, None),
        P("rows", "cols"),
        P("rows", "cols"),
        P("rows", "cols"),
        P("cols", None),
        P(None, "cols"),
        P(None, "cols"),
    )
    return jax.shard_map(
        local,
        mesh=mesh,
        in_specs=placed,
        out_specs=(P("rows", None), P("cols", None)),
        check_vma=False,
    )
```

profile of v0, /device:TPU:65, one launch (start us, length us, event | category | flops | bytes accessed | tf_op | source)
XLA Modules:
  0.0 500.2 jit_solution(12547211673845322062)
XLA Ops:
  7.3 0.7 mul.557
  8.0 0.1 mul.558
  8.2 0.7 mul.541
  8.8 0.1 mul.542
  8.9 0.7 mul.525
  9.6 0.1 mul.526
  9.7 0.7 mul.509
  10.4 0.7 mul.493
  11.1 0.1 mul.494
  11.2 0.1 mul.476
  11.3 0.7 mul.478
  12.0 0.1 mul.479
  12.1 0.7 mul.468
  12.9 0.1 copy.29
  13.8 6.0 %convolution_convert_fusion.3 = bf16[128,64,128]{2,0,1:T(8,128)(2,1)S(1)} fusion(f32[64,128,128]{2,1,0:T(8,128)} %bitcast.118, f32[64,128]{1,0:T(8,128)S(1)} %broadcast_multiply_fusion, f32[64,128]{1,0:T(8,128)S(1)} %copy.31), kind=kOutput, calls=%fused_computation.50 | convolution fusion | flops 1611694080 | bytes 6356992 | tf_op jit(solution)/shard_map/ij,bjn->bin/dot_general | solution.py:78
  19.9 1.7 convolution_convert_fusion.2
  21.6 2.3 reshape.406
  23.9 6.8 %all-to-all-start = ((bf16[16,512,128]{2,1,0:T(8,128)(2,1)}), bf16[16,512,128]{2,1,0:T(8,128)(2,1)S(1)}, u32[]{:S(2)}, u32[]{:S(2)}) async-start(bf16[16,512,128]{2,1,0:T(8,128)(2,1)} %reshape.406), calls=%async_computation | async-start | bytes 4194304 | tf_op jit(solution)/shard_map/all_to_all | solution.py:87
  30.7 0.5 all-reduce.3.cloned.1.call-start
  31.9 29.3 %all-to-all-done = bf16[16,512,128]{2,1,0:T(8,128)(2,1)S(1)} async-done(((bf16[16,512,128]{2,1,0:T(8,128)(2,1)}), bf16[16,512,128]{2,1,0:T(8,128)(2,1)S(1)}, u32[]{:S(2)}, u32[]{:S(2)}) %all-to-all-start) | async-done | bytes 2097184 | tf_op jit(solution)/shard_map/all_to_all | solution.py:87
  61.2 2.3 reshape.407
  63.4 5.1 %fusion.25 = bf16[48,8,128,128]{3,1,2,0:T(8,128)(2,1)S(1)} fusion(bf16[64,16384]{1,0:T(8,128)(2,1)} %reshape.407, s32[384]{0:T(512)S(1)} %reduce.1), kind=kOutput, calls=%fused_computation.28 | convolution fusion | flops 811622400 | bytes 14681600 | tf_op jit(solution)/shard_map/dot_general | solution.py:96
  68.5 6.5 %copy.49 = bf16[48,8,128,128]{3,2,1,0:T(8,128)(2,1)} copy(bf16[48,8,128,128]{3,1,2,0:T(8,128)(2,1)S(1)} %fusion.25) | data formatting | bytes 25165824
  75.0 22.1 %fusion.8 = f32[384,128,128]{1,2,0:T(8,128)} fusion(bf16[384,128,128]{2,1,0:T(8,128)(2,1)} %bitcast.116, bf16[1,384,128,128]{3,2,1,0:T(8,128)(2,1)} %param.23), kind=kOutput, calls=%fused_computation.11 | convolution fusion | flops 1610612736 | bytes 50331648 | tf_op jit(solution)/shard_map/kij,kjn->kin/dot_general | solution.py:98
  97.1 25.0 %copy.33 = f32[384,128,128]{0,2,1:T(8,128)} copy(f32[384,128,128]{1,2,0:T(8,128)} %fusion.8) | data formatting | bytes 50331648 | tf_op jit(solution)/shard_map/kij,kjn->kin/dot_general | solution.py:98
  122.1 27.2 %fusion.2 = f32[32,128,128]{2,0,1:T(8,128)} fusion(f32[384,128,128]{0,2,1:T(8,128)} %copy.33, f32[384]{0:T(512)S(1)} %fusion.70, s32[384]{0:T(512)S(1)} %reduce), kind=kOutput, calls=%fused_computation.2 | convolution fusion | flops 2415943680 | bytes 27266048 | tf_op jit(solution)/shard_map/dot_general | solution.py:100
  149.4 88.7 %all-reduce.3.cloned.1.call-done = f32[32,128,128]{2,0,1:T(8,128)} async-done(((f32[32,128,128]{2,0,1:T(8,128)}), f32[32,128,128]{2,0,1:T(8,128)}) %all-reduce.3.cloned.1.call-update) | async-done | bytes 2097168 | tf_op jit(solution)/shard_map/psum | solution.py:104
  238.1 9.7 %fusion.26 = bf16[48,8,128,128]{3,1,2,0:T(8,128)(2,1)} fusion(s32[384]{0:T(512)S(1)} %reduce, f32[32,128,128]{2,0,1:T(8,128)} %all-reduce.3.cloned.1.call-done), kind=kOutput, calls=%fused_computation.29 | convolution fusion | flops 409481216 | bytes 14681600 | tf_op jit(solution)/shard_map/dot_general | solution.py:108
  247.8 12.0 %copy.50 = bf16[48,8,128,128]{3,2,1,0:T(8,128)(2,1)} copy(bf16[48,8,128,128]{3,1,2,0:T(8,128)(2,1)} %fusion.26) | data formatting | bytes 25165824
  259.8 13.2 %fusion.11 = f32[384,128,128]{1,2,0:T(8,128)} fusion(bf16[384,128,128]{2,1,0:T(8,128)(2,1)} %bitcast.117, bf16[1,384,128,128]{3,2,1,0:T(8,128)(2,1)S(1)} %bitcast.115), kind=kOutput, calls=%fused_computation.12 | convolution fusion | flops 1610612736 | bytes 50331648 | tf_op jit(solution)/shard_map/kij,kin->kjn/dot_general | solution.py:110
  273.0 25.0 %copy.37 = f32[384,128,128]{0,2,1:T(8,128)} copy(f32[384,128,128]{1,2,0:T(8,128)} %fusion.11) | data formatting | bytes 50331648 | tf_op jit(solution)/shard_map/kij,kin->kjn/dot_general | solution.py:110
  298.0 27.9 %fusion = f32[64,128,128]{2,0,1:T(8,128)S(1)} fusion(f32[384,128,128]{0,2,1:T(8,128)} %copy.37, f32[384]{0:T(512)S(1)} %fusion.70, s32[384]{0:T(512)S(1)} %reduce.1), kind=kOutput, calls=%fused_computation | convolution fusion | flops 4831887360 | bytes 29363200 | tf_op jit(solution)/shard_map/dot_general | solution.py:114
  325.9 4.4 copy.38
  330.3 0.8 fusion.80
  331.1 2.5 collective-permute-start
  333.7 1.3 collective-permute-start.1
  335.1 65.8 %all-reduce.5.cloned.1.call-done = f32[16,512,128]{2,1,0:T(8,128)} async-done(((f32[16,512,128]{2,1,0:T(8,128)}), f32[16,512,128]{2,1,0:T(8,128)}) %all-reduce.5.cloned.1.call-update) | async-done | bytes 4194320 | tf_op jit(solution)/shard_map/psum | solution.py:121
  400.9 6.8 %all-to-all-start.1 = ((f32[16,512,128]{2,1,0:T(8,128)}), f32[16,512,128]{2,1,0:T(8,128)}, u32[]{:S(2)}, u32[]{:S(2)}) async-start(f32[16,512,128]{2,1,0:T(8,128)} %all-reduce.5.cloned.1.call-done), calls=%async_computation.1 | async-start | bytes 8388608 | tf_op jit(solution)/shard_map/all_to_all | solution.py:122
  407.7 0.1 fusion.81
  408.0 4.0 pad_maximum_fusion.1
  412.0 3.8 fusion.93
  415.7 20.2 %fusion.14 = f32[64,128,128]{2,1,0:T(8,128)} fusion(f32[64,128]{1,0:T(8,128)S(1)} %bitcast.134, s32[64,128]{1,0:T(8,128)S(1)} %get-tuple-element.7, f32[64,128]{1,0:T(8,128)S(1)} %bitcast.135, s32[64,128]{1,0:T(8,128)S(1)} %get-tuple-element.8, f32[64,128]{1,0:T(8,128)S(1)} %bitcast.133, s32[64,128]{1,0:T(8,128)S(1)} %get-tuple-element.9, ...), kind=kOutput, calls=%fused_computation.13 | convolution fusion | flops 3244294144 | bytes 12845056 | tf_op jit(solution)/shard_map/bij,bjn->bin/dot_general | solution.py:56
  435.9 2.5 copy.34
  438.4 34.3 %all-to-all-done.1 = f32[16,512,128]{2,1,0:T(8,128)} async-done(((f32[16,512,128]{2,1,0:T(8,128)}), f32[16,512,128]{2,1,0:T(8,128)}, u32[]{:S(2)}, u32[]{:S(2)}) %all-to-all-start.1) | async-done | bytes 4194336 | tf_op jit(solution)/shard_map/all_to_all | solution.py:122
  472.7 4.9 reshape.415
  477.6 4.6 fusion.27
  482.3 6.3 %fusion.30 = f32[64,128,128]{1,2,0:T(8,128)S(1)} fusion(f32[64,128,128]{2,0,1:T(8,128)S(1)} %fusion.27, f32[64,128]{1,0:T(8,128)S(1)} %broadcast_multiply_fusion, f32[64,128]{1,0:T(8,128)S(1)} %copy.31), kind=kOutput, calls=%fused_computation.37 | convolution fusion | flops 1610645504 | bytes 8454144 | tf_op jit(solution)/shard_map/ji,bjn->bin/dot_general | solution.py:66
  488.6 4.6 bitcast_add_fusion
  (68 shorter events, 1.5 us)
Async XLA Ops:
  7.2 12.7 %copy-start.5 = (s32[1,64]{1,0:T(1,128)S(1)}, s32[1,64]{1,0:T(1,128)}, u32[]{:S(2)}) copy-start(s32[1,64]{1,0:T(1,128)} %param.27) | copy-start | bytes 772
  21.6 10.3 %copy-start.6 = (s32[1,384]{1,0:T(1,128)S(1)}, s32[1,384]{1,0:T(1,128)}, u32[]{:S(2)}) copy-start(s32[1,384]{1,0:T(1,128)} %param.25) | copy-start | bytes 4612
  21.6 10.3 %copy-start.7 = (s32[1,384]{1,0:T(1,128)S(1)}, s32[1,384]{1,0:T(1,128)}, u32[]{:S(2)}) copy-start(s32[1,384]{1,0:T(1,128)} %param.24) | copy-start | bytes 4612
  23.9 37.3 %all-to-all-start = ((bf16[16,512,128]{2,1,0:T(8,128)(2,1)}), bf16[16,512,128]{2,1,0:T(8,128)(2,1)S(1)}, u32[]{:S(2)}, u32[]{:S(2)}) async-start(bf16[16,512,128]{2,1,0:T(8,128)(2,1)} %reshape.406), calls=%async_computation | async-start | bytes 4194304 | tf_op jit(solution)/shard_map/all_to_all | solution.py:87
  30.7 207.4 %all-reduce.3.cloned.1.call-start = ((), (), s32[]{:S(2)}) async-start(), calls=%async_computation.2 | async-start | bytes 4194304 | tf_op jit(solution)/shard_map/psum | solution.py:104
  149.3 251.6 %all-reduce.5.cloned.1.call-start = ((), (), s32[]{:S(2)}) async-start(), calls=%async_computation.3 | async-start | bytes 8388608 | tf_op jit(solution)/shard_map/psum | solution.py:121
  238.1 21.7 %slice-start = ((s8[12582912]{0:T(1024)(128)(4,1)}), s8[4194304]{0:T(1024)(128)(4,1)S(1)}, s32[]{:S(2)}) async-start(s8[12582912]{0:T(1024)(128)(4,1)} %bitcast.114), calls=%async_computation.4 | async-start | bytes 8388608
  238.1 21.7 %slice-start.1 = ((s8[12582912]{0:T(1024)(128)(4,1)}), s8[4194304]{0:T(1024)(128)(4,1)S(1)}, s32[]{:S(2)}) async-start(s8[12582912]{0:T(1024)(128)(4,1)} %bitcast.114), calls=%async_computation.5 | async-start | bytes 8388608
  247.8 12.0 %slice-start.2 = ((s8[12582912]{0:T(1024)(128)(4,1)}), s8[4194304]{0:T(1024)(128)(4,1)S(1)}, s32[]{:S(2)}) async-start(s8[12582912]{0:T(1024)(128)(4,1)} %bitcast.114), calls=%async_computation.6 | async-start | bytes 8388608
  330.3 4.7 copy-start.4
  331.1 76.8 %collective-permute-start = (f32[64,128]{1,0:T(8,128)S(1)}, f32[64,128]{1,0:T(8,128)S(1)}, u32[]{:S(2)}, u32[]{:S(2)}) collective-permute-start(f32[64,128]{1,0:T(8,128)S(1)} %get-tuple-element.4), channel_id=1, source_target_pairs={{0,1},{1,2},{2,3},{3,4},{4,5},{5,6},{6,7},{7,8},{8,9},{9,10},{10,1... | collective-permute-start | bytes 98312 | tf_op jit(solution)/shard_map/ppermute | solution.py:17
  333.7 74.3 %collective-permute-start.1 = (f32[64,128]{1,0:T(8,128)S(1)}, f32[64,128]{1,0:T(8,128)S(1)}, u32[]{:S(2)}, u32[]{:S(2)}) collective-permute-start(f32[64,128]{1,0:T(8,128)S(1)} %get-tuple-element.5), channel_id=1, source_target_pairs={{1,0},{2,1},{3,2},{4,3},{5,4},{6,5},{7,6},{8,7},{9,8},{10,9},{11,1... | collective-permute-start | bytes 98312 | tf_op jit(solution)/shard_map/ppermute | solution.py:20
  335.1 72.6 %copy-start.3 = (f32[4,8192]{1,0:T(4,128)S(1)}, f32[4,8192]{1,0:T(4,128)}, u32[]{:S(2)}) copy-start(f32[4,8192]{1,0:T(4,128)} %param.29) | copy-start | bytes 393220
  400.9 71.8 %all-to-all-start.1 = ((f32[16,512,128]{2,1,0:T(8,128)}), f32[16,512,128]{2,1,0:T(8,128)}, u32[]{:S(2)}, u32[]{:S(2)}) async-start(f32[16,512,128]{2,1,0:T(8,128)} %all-reduce.5.cloned.1.call-done), calls=%async_computation.1 | async-start | bytes 8388608 | tf_op jit(solution)/shard_map/all_to_all | solution.py:122
  415.7 20.2 %copy-start.1 = (f32[32,128,128]{2,0,1:T(8,128)S(1)}, f32[32,128,128]{2,0,1:T(8,128)}, u32[]{:S(2)}) copy-start(f32[32,128,128]{2,0,1:T(8,128)} %all-reduce.3.cloned.1.call-done) | copy-start | bytes 6291460
  482.3 6.3 %copy-start = (f32[8192,128]{1,0:T(8,128)S(1)}, f32[8192,128]{1,0:T(8,128)}, u32[]{:S(2)}) copy-start(f32[8192,128]{1,0:T(8,128)} %param.22) | copy-start | bytes 12582916
  482.3 6.3 %copy-start.2 = (f32[64,128,128]{2,1,0:T(8,128)S(1)}, f32[64,128,128]{2,1,0:T(8,128)}, u32[]{:S(2)}) copy-start(f32[64,128,128]{2,1,0:T(8,128)} %fusion.14) | copy-start | bytes 12582916
Sparse Core Ops, SparseCore 0:
  149.4 88.5 all-reduce.2
  330.4 70.4 all-reduce.4
where the time goes:
time: 507 us; the launch traced here: 500 us
  waiting for transfers between devices  218 us (43%)
  matrix products  144 us (28%)
  local copies, waits for them, and re-layouts  91.8 us (18%)
  starting transfers between devices  17.9 us (4%)
  between operations  15.3 us (3%)
  other arithmetic  13.2 us (3%)
    psum x1, waiting for transfers between devices, local(): predicted = lax.psum(partial_rows, 'cols')  88.7 us
    psum x1, waiting for transfers between devices, local(): summed = lax.psum(partial_cols, 'rows')  65.8 us
    all_to_all x1, waiting for transfers between devices, local(): lax.all_to_all(summed.reshape(col_devices, per_peer * BLK, vec_width), 'c...  34.3 us
    all_to_all x1, waiting for transfers between devices, local(): lax.all_to_all(outgoing, 'cols', split_axis=0, concat_axis=0, tiled=True)  29.3 us
    dot_general x1, matrix products, local(): jnp.dot(col_mask, adjoint.reshape(slot_count, BLK * vec_width), precision...  27.9 us
    dot_general x1, matrix products, local(): jnp.dot(row_mask, forward.reshape(slot_count, BLK * vec_width), precision...  27.2 us
    dot_general x1, local copies, waits for them, and re-layouts, local(): jnp.einsum('kij,kin->kjn', sensors, chosen, preferred_element_type=jnp.fl...  25 us
    dot_general x1, local copies, waits for them, and re-layouts, local(): jnp.einsum('kij,kjn->kin', sensors, picked, preferred_element_type=jnp.fl...  25 us
  transfers between devices with their start and end apart: 6, of which 4 were waited for; matrix products, arithmetic and copies ran while one was open for 6% of the time, Pallas kernels for 0%

commit v1 on v0

--- a/solution.py
+++ b/solution.py
@@ -101,7 +101,11 @@
         row_mask, forward.reshape(slot_count, BLK * vec_width), precision=highest
     )
     partial_rows = partial_rows.reshape(RB_DEV, BLK, vec_width)
-    predicted = lax.psum(partial_rows, "cols")
+    predicted = partial_rows
+    for hop in (1, 2, 4, 8):
+        predicted = predicted + lax.ppermute(
+            predicted, "cols", [(dev, dev ^ hop) for dev in range(16)]
+        )
     data_image = predicted.reshape(RB_DEV * BLK, vec_width)
     image_half = predicted.astype(jnp.bfloat16).reshape(RB_DEV, BLK * vec_width)
     pick_rows = one_hot(rows_here, RB_DEV, jnp.bfloat16)

time: 507 us -> 604 us (1.19)
  waiting for transfers between devices: 218 us -> 310 us
  starting transfers between devices: 17.9 us -> 24.2 us
    ppermute x0 -> x4, waiting for transfers between devices: none -> 174 us  [local(): lax.ppermute(predicted, 'cols', [(dev, dev ^ hop) for dev in range(16)])]
    psum x1 -> x0, waiting for transfers between devices: 88.7 us -> none  [local(): predicted = lax.psum(partial_rows, 'cols')]
    ppermute x0 -> x4, starting transfers between devices: none -> 7.78 us  [local(): lax.ppermute(predicted, 'cols', [(dev, dev ^ hop) for dev in range(16)])]
    psum x1, waiting for transfers between devices: 65.8 us -> 72.2 us  [local(): summed = lax.psum(partial_cols, 'rows')]
  transfers between devices with their start and end apart: 6 -> 9, of which waited for: 4 -> 7; matrix products, arithmetic and copies ran while one was open for 6% -> 5% of each run, Pallas kernels for 0% -> 0%
where the time goes in v1:
time: 604 us; the launch traced here: 598 us
  waiting for transfers between devices  310 us (51%)
  matrix products  140 us (23%)
  local copies, waits for them, and re-layouts  92 us (15%)
  starting transfers between devices  24.2 us (4%)
  other arithmetic  16.5 us (3%)
  between operations  15.4 us (3%)
    ppermute x4, waiting for transfers between devices, local(): lax.ppermute(predicted, 'cols', [(dev, dev ^ hop) for dev in range(16)])  174 us
    psum x1, waiting for transfers between devices, local(): summed = lax.psum(partial_cols, 'rows')  72.2 us
    all_to_all x1, waiting for transfers between devices, local(): lax.all_to_all(summed.reshape(col_devices, per_peer * BLK, vec_width), 'c...  34.5 us
    all_to_all x1, waiting for transfers between devices, local(): lax.all_to_all(outgoing, 'cols', split_axis=0, concat_axis=0, tiled=True)  29.2 us
    dot_general x1, matrix products, local(): jnp.dot(col_mask, adjoint.reshape(slot_count, BLK * vec_width), precision...  28.1 us
    dot_general x1, matrix products, local(): jnp.dot(row_mask, forward.reshape(slot_count, BLK * vec_width), precision...  26.3 us
    dot_general x1, local copies, waits for them, and re-layouts, local(): jnp.einsum('kij,kin->kjn', sensors, chosen, preferred_element_type=jnp.fl...  24.9 us
    dot_general x1, local copies, waits for them, and re-layouts, local(): jnp.einsum('kij,kjn->kin', sensors, picked, preferred_element_type=jnp.fl...  24.9 us
  transfers between devices with their start and end apart: 9, of which 7 were waited for; matrix products, arithmetic and copies ran while one was open for 5% of the time, Pallas kernels for 0%

profile of v1, /device:TPU:65, one launch (start us, length us, event | category | flops | bytes accessed | tf_op | source)
XLA Modules:
  0.0 598.1 jit_solution(17836447287611784091)
XLA Ops:
  7.3 0.7 mul.557
  8.2 0.7 mul.541
  8.9 0.7 mul.525
  9.7 0.7 mul.509
  10.4 0.7 mul.493
  11.3 0.7 mul.478
  12.1 0.7 mul.468
  13.8 6.0 %convolution_convert_fusion.3 = bf16[128,64,128]{2,0,1:T(8,128)(2,1)S(1)} fusion(f32[64,128,128]{2,1,0:T(8,128)} %bitcast.116, f32[64,128]{1,0:T(8,128)S(1)} %broadcast_multiply_fusion, f32[64,128]{1,0:T(8,128)S(1)} %copy.31), kind=kOutput, calls=%fused_computation.50 | convolution fusion | flops 1611694080 | bytes 6356992 | tf_op jit(solution)/shard_map/ij,bjn->bin/dot_general | solution.py:78
  19.9 1.7 convolution_convert_fusion.2
  21.6 2.3 reshape.406
  23.9 6.7 %all-to-all-start = ((bf16[16,512,128]{2,1,0:T(8,128)(2,1)}), bf16[16,512,128]{2,1,0:T(8,128)(2,1)S(1)}, u32[]{:S(2)}, u32[]{:S(2)}) async-start(bf16[16,512,128]{2,1,0:T(8,128)(2,1)} %reshape.406), calls=%async_computation | async-start | bytes 4194304 | tf_op jit(solution)/shard_map/all_to_all | solution.py:87
  30.7 0.6 all-reduce.2.cloned.1.call-start
  32.0 29.2 %all-to-all-done = bf16[16,512,128]{2,1,0:T(8,128)(2,1)S(1)} async-done(((bf16[16,512,128]{2,1,0:T(8,128)(2,1)}), bf16[16,512,128]{2,1,0:T(8,128)(2,1)S(1)}, u32[]{:S(2)}, u32[]{:S(2)}) %all-to-all-start) | async-done | bytes 2097184 | tf_op jit(solution)/shard_map/all_to_all | solution.py:87
  61.2 2.3 reshape.407
  63.4 5.1 fusion.25
  68.5 6.6 %copy.49 = bf16[48,8,128,128]{3,2,1,0:T(8,128)(2,1)} copy(bf16[48,8,128,128]{3,1,2,0:T(8,128)(2,1)S(1)} %fusion.25) | data formatting | bytes 25165824
  75.1 22.1 %fusion.8 = f32[384,128,128]{1,2,0:T(8,128)} fusion(bf16[384,128,128]{2,1,0:T(8,128)(2,1)} %bitcast.114, bf16[1,384,128,128]{3,2,1,0:T(8,128)(2,1)} %param.23), kind=kOutput, calls=%fused_computation.11 | convolution fusion | flops 1610612736 | bytes 50331648 | tf_op jit(solution)/shard_map/kij,kjn->kin/dot_general | solution.py:98
  97.2 24.9 %copy.33 = f32[384,128,128]{0,2,1:T(8,128)} copy(f32[384,128,128]{1,2,0:T(8,128)} %fusion.8) | data formatting | bytes 50331648 | tf_op jit(solution)/shard_map/kij,kjn->kin/dot_general | solution.py:98
  122.1 26.3 %fusion.2 = f32[32,128,128]{2,0,1:T(8,128)S(1)} fusion(f32[384,128,128]{0,2,1:T(8,128)} %copy.33, f32[384]{0:T(512)S(1)} %fusion.70, s32[384]{0:T(512)S(1)} %reduce), kind=kOutput, calls=%fused_computation.2 | convolution fusion | flops 2415943680 | bytes 27266048 | tf_op jit(solution)/shard_map/dot_general | solution.py:100
  148.5 45.0 %collective-permute-done = f32[32,128,128]{2,0,1:T(8,128)S(1)} collective-permute-done((f32[32,128,128]{2,0,1:T(8,128)S(1)}, f32[32,128,128]{2,0,1:T(8,128)S(1)}, u32[]{:S(2)}, u32[]{:S(2)}) %collective-permute-start) | collective-permute-done | bytes 2097184 | tf_op jit(solution)/shard_map/ppermute | solution.py:106
  193.5 0.5 add.27
  194.0 2.7 collective-permute-start.1
  196.7 43.6 %collective-permute-done.1 = f32[32,128,128]{2,0,1:T(8,128)S(1)} collective-permute-done((f32[32,128,128]{2,0,1:T(8,128)S(1)}, f32[32,128,128]{2,0,1:T(8,128)S(1)}, u32[]{:S(2)}, u32[]{:S(2)}) %collective-permute-start.1) | collective-permute-done | bytes 2097184 | tf_op jit(solution)/shard_map/ppermute | solution.py:106
  240.8 1.5 collective-permute-start.2
  242.3 42.2 %collective-permute-done.2 = f32[32,128,128]{2,0,1:T(8,128)S(1)} collective-permute-done((f32[32,128,128]{2,0,1:T(8,128)S(1)}, f32[32,128,128]{2,0,1:T(8,128)S(1)}, u32[]{:S(2)}, u32[]{:S(2)}) %collective-permute-start.2) | collective-permute-done | bytes 2097184 | tf_op jit(solution)/shard_map/ppermute | solution.py:106
  285.0 3.5 collective-permute-start.3
  288.5 43.1 %collective-permute-done.3 = f32[32,128,128]{2,0,1:T(8,128)S(1)} collective-permute-done((f32[32,128,128]{2,0,1:T(8,128)S(1)}, f32[32,128,128]{2,0,1:T(8,128)S(1)}, u32[]{:S(2)}, u32[]{:S(2)}) %collective-permute-start.3) | collective-permute-done | bytes 2097184 | tf_op jit(solution)/shard_map/ppermute | solution.py:106
  331.6 1.8 convert_bitcast_fusion
  333.4 6.5 %fusion.26 = bf16[48,8,128,128]{3,1,2,0:T(8,128)(2,1)} fusion(bf16[128,4,8,128]{3,2,1,0:T(8,128)(2,1)S(1)} %get-tuple-element.2, s32[384]{0:T(512)S(1)} %reduce), kind=kOutput, calls=%fused_computation.29 | convolution fusion | flops 408956928 | bytes 13633024 | tf_op jit(solution)/shard_map/dot_general | solution.py:112
  339.9 12.0 %copy.50 = bf16[48,8,128,128]{3,2,1,0:T(8,128)(2,1)} copy(bf16[48,8,128,128]{3,1,2,0:T(8,128)(2,1)} %fusion.26) | data formatting | bytes 25165824
  351.9 13.2 %fusion.11 = f32[384,128,128]{1,2,0:T(8,128)} fusion(bf16[384,128,128]{2,1,0:T(8,128)(2,1)} %bitcast.115, bf16[1,384,128,128]{3,2,1,0:T(8,128)(2,1)S(1)} %bitcast.113), kind=kOutput, calls=%fused_computation.12 | convolution fusion | flops 1610612736 | bytes 50331648 | tf_op jit(solution)/shard_map/kij,kin->kjn/dot_general | solution.py:114
  365.2 24.9 %copy.37 = f32[384,128,128]{0,2,1:T(8,128)} copy(f32[384,128,128]{1,2,0:T(8,128)} %fusion.11) | data formatting | bytes 50331648 | tf_op jit(solution)/shard_map/kij,kin->kjn/dot_general | solution.py:114
  390.1 28.1 %fusion = f32[64,128,128]{2,0,1:T(8,128)S(1)} fusion(f32[384,128,128]{0,2,1:T(8,128)} %copy.37, f32[384]{0:T(512)S(1)} %fusion.70, s32[384]{0:T(512)S(1)} %reduce.1), kind=kOutput, calls=%fused_computation | convolution fusion | flops 4831887360 | bytes 29363200 | tf_op jit(solution)/shard_map/dot_general | solution.py:118
  418.2 4.4 copy.38
  422.6 0.8 fusion.80
  423.5 1.3 collective-permute-start.4
  424.7 1.3 collective-permute-start.5
  426.2 72.2 %all-reduce.2.cloned.1.call-done = f32[16,512,128]{2,1,0:T(8,128)} async-done(((f32[16,512,128]{2,1,0:T(8,128)}), f32[16,512,128]{2,1,0:T(8,128)}) %all-reduce.2.cloned.1.call-update) | async-done | bytes 4194320 | tf_op jit(solution)/shard_map/psum | solution.py:125
  498.4 6.6 %all-to-all-start.1 = ((f32[16,512,128]{2,1,0:T(8,128)}), f32[16,512,128]{2,1,0:T(8,128)}, u32[]{:S(2)}, u32[]{:S(2)}) async-start(f32[16,512,128]{2,1,0:T(8,128)} %all-reduce.2.cloned.1.call-done), calls=%async_computation.1 | async-start | bytes 8388608 | tf_op jit(solution)/shard_map/all_to_all | solution.py:126
  505.3 4.0 pad_maximum_fusion.1
  509.2 3.8 fusion.93
  513.0 20.2 %fusion.14 = f32[64,128,128]{2,1,0:T(8,128)} fusion(f32[64,128]{1,0:T(8,128)S(1)} %bitcast.132, s32[64,128]{1,0:T(8,128)S(1)} %get-tuple-element.9, f32[64,128]{1,0:T(8,128)S(1)} %bitcast.133, s32[64,128]{1,0:T(8,128)S(1)} %get-tuple-element.10, f32[64,128]{1,0:T(8,128)S(1)} %bitcast.131, s32[64,128]{1,0:T(8,128)S(1)} %get-tuple-element.11, ...), kind=kOutput, calls=%fused_computation.13 | convolution fusion | flops 3244294144 | bytes 12845056 | tf_op jit(solution)/shard_map/bij,bjn->bin/dot_general | solution.py:56
  533.2 2.5 copy.34
  535.7 34.5 %all-to-all-done.1 = f32[16,512,128]{2,1,0:T(8,128)} async-done(((f32[16,512,128]{2,1,0:T(8,128)}), f32[16,512,128]{2,1,0:T(8,128)}, u32[]{:S(2)}, u32[]{:S(2)}) %all-to-all-start.1) | async-done | bytes 4194336 | tf_op jit(solution)/shard_map/all_to_all | solution.py:126
  570.2 5.2 reshape.415
  575.4 4.6 fusion.27
  580.0 6.3 %fusion.30 = f32[64,128,128]{1,2,0:T(8,128)S(1)} fusion(f32[64,128,128]{2,0,1:T(8,128)S(1)} %fusion.27, f32[64,128]{1,0:T(8,128)S(1)} %broadcast_multiply_fusion, f32[64,128]{1,0:T(8,128)S(1)} %copy.31), kind=kOutput, calls=%fused_computation.37 | convolution fusion | flops 1610645504 | bytes 8454144 | tf_op jit(solution)/shard_map/ji,bjn->bin/dot_general | solution.py:66
  586.4 4.6 bitcast_add_fusion
  (77 shorter events, 3.3 us)
Async XLA Ops:
  7.2 12.7 %copy-start.5 = (s32[1,64]{1,0:T(1,128)S(1)}, s32[1,64]{1,0:T(1,128)}, u32[]{:S(2)}) copy-start(s32[1,64]{1,0:T(1,128)} %param.27) | copy-start | bytes 772
  21.6 10.3 %copy-start.6 = (s32[1,384]{1,0:T(1,128)S(1)}, s32[1,384]{1,0:T(1,128)}, u32[]{:S(2)}) copy-start(s32[1,384]{1,0:T(1,128)} %param.25) | copy-start | bytes 4612
  21.6 10.4 %copy-start.7 = (s32[1,384]{1,0:T(1,128)S(1)}, s32[1,384]{1,0:T(1,128)}, u32[]{:S(2)}) copy-start(s32[1,384]{1,0:T(1,128)} %param.24) | copy-start | bytes 4612
  23.9 37.2 %all-to-all-start = ((bf16[16,512,128]{2,1,0:T(8,128)(2,1)}), bf16[16,512,128]{2,1,0:T(8,128)(2,1)S(1)}, u32[]{:S(2)}, u32[]{:S(2)}) async-start(bf16[16,512,128]{2,1,0:T(8,128)(2,1)} %reshape.406), calls=%async_computation | async-start | bytes 4194304 | tf_op jit(solution)/shard_map/all_to_all | solution.py:87
  30.7 467.8 %all-reduce.2.cloned.1.call-start = ((), (), s32[]{:S(2)}) async-start(), calls=%async_computation.2 | async-start | bytes 8388608 | tf_op jit(solution)/shard_map/psum | solution.py:125
  148.4 45.1 %collective-permute-start = (f32[32,128,128]{2,0,1:T(8,128)S(1)}, f32[32,128,128]{2,0,1:T(8,128)S(1)}, u32[]{:S(2)}, u32[]{:S(2)}) collective-permute-start(f32[32,128,128]{2,0,1:T(8,128)S(1)} %fusion.2), channel_id=1, source_target_pairs={{0,1},{1,0},{2,3},{3,2},{4,5},{5,4},{6,7},{7,6},{8,9},{9,8},{10,11... | collective-permute-start | bytes 6291464 | tf_op jit(solution)/shard_map/ppermute | solution.py:106
  194.0 46.3 %collective-permute-start.1 = (f32[32,128,128]{2,0,1:T(8,128)S(1)}, f32[32,128,128]{2,0,1:T(8,128)S(1)}, u32[]{:S(2)}, u32[]{:S(2)}) collective-permute-start(f32[32,128,128]{2,0,1:T(8,128)S(1)} %add.27), channel_id=1, source_target_pairs={{0,2},{1,3},{2,0},{3,1},{4,6},{5,7},{6,4},{7,5},{8,10},{9,11},{10,... | collective-permute-start | bytes 6291464 | tf_op jit(solution)/shard_map/ppermute | solution.py:106
  240.8 43.7 %collective-permute-start.2 = (f32[32,128,128]{2,0,1:T(8,128)S(1)}, f32[32,128,128]{2,0,1:T(8,128)S(1)}, u32[]{:S(2)}, u32[]{:S(2)}) collective-permute-start(f32[32,128,128]{2,0,1:T(8,128)S(1)} %add.28), channel_id=1, source_target_pairs={{0,4},{1,5},{2,6},{3,7},{4,0},{5,1},{6,2},{7,3},{8,12},{9,13},{10,... | collective-permute-start | bytes 6291464 | tf_op jit(solution)/shard_map/ppermute | solution.py:106
  285.0 46.6 %collective-permute-start.3 = (f32[32,128,128]{2,0,1:T(8,128)S(1)}, f32[32,128,128]{2,0,1:T(8,128)S(1)}, u32[]{:S(2)}, u32[]{:S(2)}) collective-permute-start(f32[32,128,128]{2,0,1:T(8,128)S(1)} %add.29), channel_id=1, source_target_pairs={{0,8},{1,9},{2,10},{3,11},{4,12},{5,13},{6,14},{7,15},{8,0},{9,1},... | collective-permute-start | bytes 6291464 | tf_op jit(solution)/shard_map/ppermute | solution.py:106
  333.4 18.5 %slice-start = ((s8[12582912]{0:T(1024)(128)(4,1)}), s8[4194304]{0:T(1024)(128)(4,1)S(1)}, s32[]{:S(2)}) async-start(s8[12582912]{0:T(1024)(128)(4,1)} %bitcast.112), calls=%async_computation.3 | async-start | bytes 8388608
  333.4 18.5 %slice-start.1 = ((s8[12582912]{0:T(1024)(128)(4,1)}), s8[4194304]{0:T(1024)(128)(4,1)S(1)}, s32[]{:S(2)}) async-start(s8[12582912]{0:T(1024)(128)(4,1)} %bitcast.112), calls=%async_computation.4 | async-start | bytes 8388608
  339.9 12.0 %slice-start.2 = ((s8[12582912]{0:T(1024)(128)(4,1)}), s8[4194304]{0:T(1024)(128)(4,1)S(1)}, s32[]{:S(2)}) async-start(s8[12582912]{0:T(1024)(128)(4,1)} %bitcast.112), calls=%async_computation.5 | async-start | bytes 8388608
  422.6 3.4 copy-start.4
  423.5 81.8 %collective-permute-start.4 = (f32[64,128]{1,0:T(8,128)S(1)}, f32[64,128]{1,0:T(8,128)S(1)}, u32[]{:S(2)}, u32[]{:S(2)}) collective-permute-start(f32[64,128]{1,0:T(8,128)S(1)} %get-tuple-element.6), channel_id=1, source_target_pairs={{0,1},{1,2},{2,3},{3,4},{4,5},{5,6},{6,7},{7,8},{8,9},{9,10},{10,1... | collective-permute-start | bytes 98312 | tf_op jit(solution)/shard_map/ppermute | solution.py:17
  424.7 80.5 %collective-permute-start.5 = (f32[64,128]{1,0:T(8,128)S(1)}, f32[64,128]{1,0:T(8,128)S(1)}, u32[]{:S(2)}, u32[]{:S(2)}) collective-permute-start(f32[64,128]{1,0:T(8,128)S(1)} %get-tuple-element.7), channel_id=1, source_target_pairs={{1,0},{2,1},{3,2},{4,3},{5,4},{6,5},{7,6},{8,7},{9,8},{10,9},{11,1... | collective-permute-start | bytes 98312 | tf_op jit(solution)/shard_map/ppermute | solution.py:20
  426.2 78.8 %copy-start.3 = (f32[4,8192]{1,0:T(4,128)S(1)}, f32[4,8192]{1,0:T(4,128)}, u32[]{:S(2)}) copy-start(f32[4,8192]{1,0:T(4,128)} %param.29) | copy-start | bytes 393220
  498.4 71.8 %all-to-all-start.1 = ((f32[16,512,128]{2,1,0:T(8,128)}), f32[16,512,128]{2,1,0:T(8,128)}, u32[]{:S(2)}, u32[]{:S(2)}) async-start(f32[16,512,128]{2,1,0:T(8,128)} %all-reduce.2.cloned.1.call-done), calls=%async_computation.1 | async-start | bytes 8388608 | tf_op jit(solution)/shard_map/all_to_all | solution.py:126
  513.0 20.2 %copy-start.1 = (f32[32,128,128]{2,0,1:T(8,128)S(1)}, f32[32,128,128]{2,0,1:T(8,128)}, u32[]{:S(2)}) copy-start(f32[32,128,128]{2,0,1:T(8,128)} %get-tuple-element.3) | copy-start | bytes 6291460
  580.0 6.3 %copy-start = (f32[8192,128]{1,0:T(8,128)S(1)}, f32[8192,128]{1,0:T(8,128)}, u32[]{:S(2)}) copy-start(f32[8192,128]{1,0:T(8,128)} %param.22) | copy-start | bytes 12582916
  580.0 6.3 %copy-start.2 = (f32[64,128,128]{2,1,0:T(8,128)S(1)}, f32[64,128,128]{2,1,0:T(8,128)}, u32[]{:S(2)}) copy-start(f32[64,128,128]{2,1,0:T(8,128)} %fusion.14) | copy-start | bytes 12582916
Sparse Core Ops, SparseCore 0:
  422.8 75.6 all-reduce.1
